TPU v7x, 128 devices: a whole 4x4x4 slice. The times are simulated.
128 devices in a mesh: row: 8 (over z, core), col: 16 (over y, x).
Axes of the slice: x: 4, y: 4, z: 4, core: 2. Of those that a mesh axis runs over, the one named last changes fastest.
Arguments:
- hidden: bfloat16 [1408, 16384], P('col', 'row'), may hold values from -18 to 18
- gain_in: bfloat16 [1408], replicated, may hold values from 0.5 to 1.5
- w_query: bfloat16 [1408, 1408], P('col'), may hold values from -0.3125 to 0.3125
- w_pair: bfloat16 [2, 1408, 1408], P(None, 'col'), may hold values from -0.15625 to 0.15625
- kv_cache: bfloat16 [2, 1408, 16384], P(None, 'col', 'row'), may hold values from -103 to 103
- recompute_rows: int32 [8, 200], P('row'), may hold values from 0 to 2047, as said below
- segment_ids: int32 [16384], P('row'), may hold values from -1 to 1, as said below
- w_out: bfloat16 [1408, 1408], P('col'), may hold values from -0.3125 to 0.3125
- gain_merge: bfloat16 [1408], replicated, may hold values from 0.5 to 1.5
- w_merge: bfloat16 [4, 1408, 1408], P(None, 'col'), may hold values from -0.078125 to 0.078125
- requests: int32 [8, 16, 85], P('row'), may hold values from -1 to 511, as said below
Outputs:
- delivered: bfloat16 [8, 16, 85, 1408], P('row', 'col')
Inputs may be any that keep to these rules, and one draw needn't show every extreme that they name: `segment_ids`: ids do not fall along the tokens except to -1 for the padding at the end; every image covers a multiple of 4 tokens and starts at a multiple of 4. `recompute_rows`: the 200 offsets of one index of row are distinct. `requests`: for each index of row, the lists of all owners together name each of its 512 merged tokens exactly once; unused slots hold -1 and follow the used ones.
All inputs are finite; a program needn't handle non-finite values.
Results may differ from a plain program's by a relative error of at most 0.025.
The roundings to bfloat16 on the way count: a program that leaves them out, or rounds other values in their place, can miss the bound.
Values may be sent and summed in bfloat16 or wider, within the bound.
A program may use at most 128 MiB of HBM per device.

v0:
```python
import jax
import jax.numpy as jnp
from jax import lax
from jax.sharding import PartitionSpec as P

HD = 88
EPSILON = 1e-06
MASKED = -1e30
KEY_BLOCK = 1024


def on_device(
    hidden,
    gain_in,
    w_query,
    w_pair,
    kv_cache,
    recompute_rows,
    segment_ids,
    w_out,
    gain_merge,
    w_merge,
    requests,
):
    local_width, tok_rows = hidden.shape
    model_width = w_query.shape[1]
    n_col = model_width // local_width
    heads_here = local_width // HD
    score_scale = HD ** (-0.5)
    col_index = lax.axis_index("col")
    full_rows = lax.all_gather(hidden, "col", axis=0, tiled=True)
    out_weight = lax.all_gather(w_out, "col", axis=0, tiled=True)
    full_float = full_rows.astype(jnp.float32)
    in_mean = jnp.sum(full_float, axis=0, keepdims=True) / model_width
    in_square = jnp.sum(full_float * full_float, axis=0, keepdims=True) / model_width
    normed = (
        (full_float - in_mean)
        * lax.rsqrt(in_square - in_mean * in_mean + EPSILON)
        * gain_in.astype(jnp.float32)[:, None]
    ).astype(jnp.bfloat16)
    queries = jnp.dot(w_query, normed, preferred_element_type=jnp.float32).astype(jnp.bfloat16)
    picked_rows = recompute_rows[0]
    normed_picked = jnp.take(normed, picked_rows, axis=1)
    fresh_pairs = jnp.dot(
        w_pair.reshape(2 * local_width, model_width),
        normed_picked,
        preferred_element_type=jnp.float32,
    )
    fresh_pairs = fresh_pairs.astype(jnp.bfloat16).reshape(2, local_width, -1)
    keys_values = kv_cache.at[:, :, picked_rows].set(fresh_pairs)
    query_heads = queries.reshape(heads_here, HD, tok_rows)
    pair_local = jnp.concatenate(
        [keys_values.reshape(2 * local_width, tok_rows), segment_ids.astype(jnp.bfloat16)[None, :]],
        axis=0,
    )
    pair_all = lax.all_gather(pair_local, "row", axis=1, tiled=True)
    pair_rows = pair_all[: 2 * local_width].reshape(2, local_width, -1)
    segment_line = pair_all[2 * local_width].astype(jnp.int32)

    def take_block(carried, pair_block, segment_block):
        running_max, running_sum, weighted = carried
        key_block = pair_block[0].reshape(heads_here, HD, -1)
        value_block = pair_block[1].reshape(heads_here, HD, -1)
        scores = (
            jnp.einsum("hdq,hdk->hqk", query_heads, key_block, preferred_element_type=jnp.float32)
            * score_scale
        )
        allowed = (segment_ids[:, None] == segment_block[None, :])[None, :, :]
        new_max = jnp.maximum(running_max, jnp.max(jnp.where(allowed, scores, MASKED), axis=2))
        weights_exp = jnp.where(allowed, jnp.exp(scores - new_max[:, :, None]), 0.0)
        factor = jnp.exp(running_max - new_max)
        running_sum = running_sum * factor + jnp.sum(weights_exp, axis=2)
        product = jnp.einsum(
            "hqk,hdk->hdq",
            weights_exp.astype(jnp.bfloat16),
            value_block,
            preferred_element_type=jnp.float32,
        )
        weighted = weighted * factor[:, None, :] + product
        return (new_max, running_sum, weighted)

    starting = (
        jnp.full((heads_here, tok_rows), MASKED, jnp.float32),
        jnp.zeros((heads_here, tok_rows), jnp.float32),
        jnp.zeros((heads_here, HD, tok_rows), jnp.float32),
    )
    piece_rows = pair_rows.shape[2]
    whole_blocks = piece_rows // KEY_BLOCK

    def loop_body(block_index, loop_state):
        pair_block = lax.dynamic_slice_in_dim(pair_rows, block_index * KEY_BLOCK, KEY_BLOCK, 2)
        segment_block = lax.dynamic_slice_in_dim(
            segment_line, block_index * KEY_BLOCK, KEY_BLOCK, 0
        )
        return take_block(loop_state, pair_block, segment_block)

    running_max, running_sum, weighted = lax.fori_loop(0, whole_blocks, loop_body, starting)
    attended = (
        (weighted / running_sum[:, None, :]).astype(jnp.bfloat16).reshape(local_width, tok_rows)
    )
    chunk = tok_rows // n_col
    attended_chunk = lax.all_to_all(attended, "col", 1, 0, tiled=True)
    x_chunk = lax.dynamic_slice_in_dim(full_float, col_index * chunk, chunk, 1)
    projected = lax.dot_general(
        out_weight, attended_chunk, (((0,), (0,)), ((), ())), preferred_element_type=jnp.float32
    )
    updated = x_chunk + projected
    row_mean = jnp.sum(updated, axis=0, keepdims=True) / model_width
    row_square = jnp.sum(updated * updated, axis=0, keepdims=True) / model_width
    merger_chunk = (
        (updated - row_mean)
        * lax.rsqrt(row_square - row_mean * row_mean + EPSILON)
        * gain_merge.astype(jnp.float32)[:, None]
    ).astype(jnp.bfloat16)
    merge_weight, _ = lax.optimization_barrier((w_merge, pair_all))
    merge_full = lax.all_gather(merge_weight, "col", axis=1, tiled=True)
    grouped = merger_chunk.reshape(model_width, chunk // 4, 4)
    merged_here = jnp.einsum("fgi,ifd->gd", grouped, merge_full, preferred_element_type=jnp.float32)
    merged_all = lax.all_gather(merged_here.astype(jnp.bfloat16), "col", axis=0, tiled=True)
    wanted_rows = lax.dynamic_index_in_dim(requests[0], col_index, 0, keepdims=False)
    is_valid = wanted_rows >= 0
    safe_index = jnp.where(is_valid, wanted_rows, 0)
    picked = jnp.where(is_valid[:, None], merged_all[safe_index], jnp.zeros((), jnp.bfloat16))
    return picked.reshape(1, 1, picked.shape[0], model_width)


def solution(mesh):
    placed = (
        P("col", "row"),
        P(),
        P("col", None),
        P(None, "col", None),
        P(None, "col", "row"),
        P("row", None),
        P("row"),
        P("col", None),
        P(),
        P(None, "col", None),
        P("row", None, None),
    )
    return jax.shard_map(
        on_device,
        mesh=mesh,
        in_specs=placed,
        out_specs=P("row", "col", None, None),
        check_vma=False,
    )
```

profile of v0, /device:TPU:0, one launch (start us, length us, event | category | flops | bytes accessed | tf_op | source)
XLA Modules:
  0.0 484.3 jit_solution(13265763063287293929)
XLA Ops:
  12.5 58.2 %all-gather.6.cloned.1.call-done = bf16[1408,2048]{1,0:T(8,128)(2,1)} async-done(((bf16[88,2048]{1,0:T(8,128)(2,1)}), bf16[1408,2048]{1,0:T(8,128)(2,1)}) %all-gather.6.cloned.1.call-update) | async-done | bytes 5767184 | tf_op jit(solution)/shard_map/all_gather | solution.py:31
  70.7 8.3 %copy.28 = bf16[1408,2048]{0,1:T(8,128)(2,1)} copy(bf16[1408,2048]{1,0:T(8,128)(2,1)} %all-gather.6.cloned.1.call-done) | data formatting | bytes 11534336 | tf_op jit(solution)/shard_map/all_gather | solution.py:31
  79.1 4.5 convert_reduce_fusion
  83.6 4.0 multiply_convert_fusion
  87.6 5.0 %gather_fusion = bf16[200,1408]{1,0:T(8,128)(2,1)S(1)} fusion(bf16[1408,2048]{0,1:T(8,128)(2,1)} %multiply_convert_fusion, s32[1024]{0:T(1024)S(1)} %pad_clamp_fusion.1), kind=kCustom, calls=%fused_computation | custom fusion | bytes 1127200 | tf_op jit(solution)/shard_map/jit(_take)/gather | solution.py:43
  93.2 6.9 %scatter_fusion = bf16[2,88,2048]{1,0,2:T(2,128)(2,1)S(1)} fusion(bf16[2,88,2048]{1,0,2:T(2,128)(2,1)S(1)} %copy.30, s32[200]{0:T(256)S(1)} %bitcast.122, bf16[200,2,88]{2,1,0:T(2,128)(2,1)S(1)} %bitcast.115), kind=kCustom, calls=%fused_computation.2 | custom fusion | bytes 212000 | tf_op jit(solution)/shard_map/scatter | solution.py:50
  102.8 4.7 fusion.22
  107.5 34.2 %all-gather.8.cloned.1.call-done = bf16[177,16384]{1,0:T(8,128)(2,1)} async-done(((bf16[177,2048]{1,0:T(8,128)(2,1)}), bf16[177,16384]{1,0:T(8,128)(2,1)}) %all-gather.8.cloned.1.call-update) | async-done | bytes 5799952 | tf_op jit(solution)/shard_map/all_gather | solution.py:56
  141.7 5.8 %slice.29 = bf16[176,16384]{1,0:T(8,128)(2,1)} slice(bf16[177,16384]{1,0:T(8,128)(2,1)} %all-gather.8.cloned.1.call-done), slice={[0:176], [0:16384]} | slice | bytes 11534336 | tf_op jit(solution)/shard_map/slice | solution.py:57
  148.5 254.0 %while.18 = (s32[]{:T(128)}, f32[1,2048]{1,0:T(1,128)S(1)}, f32[1,2048]{1,0:T(1,128)S(1)}, f32[1,88,2048]{2,1,0:T(8,128)S(1)}, s32[2048]{0:T(1024)S(1)}, /*index...) while((s32[]{:T(128)}, f32[1,2048]{1,0:T(1,128)S(1)}, ...), condition=%wide.region_6.7_spmd.clone, body=%wide.region_3.0_spmd.clone.sunk | while | flops 768108544 | bytes 27504848 | solution.py:97
  148.5 5.6 %fusion.45 = (f32[2048]{0:T(1024)S(1)}, f32[1024,2048]{1,0:T(8,128)}) fusion(s32[2048]{0:T(1024)S(1)} %get-tuple-element.292, s32[1024]{0:T(1024)S(1)} %dynamic_slice.32, bf16[1,88,2048]{2,1,0:T(8,128)(2,1)S(1)} %get-tuple-element.295, bf16[2,88,16384]{2,1,0:T(8,128)(2,1)} %get-tuple-element.294, s32[]{:T(128)S(6)} %select_n.132), kind=kOutput, calls=%fused_computation.5.clone.1 | convolution fusion | flops 377485312 | bytes 8949764 | tf_op jit(solution)/shard_map/while/body/eval_jaxpr/hdq,hdk->hqk/dot_general | solution.py:65
  154.1 4.6 fusion.47
  158.8 5.5 %fusion.49 = f32[1,88,2048]{2,1,0:T(8,128)S(1)} fusion(f32[1024,2048]{1,0:T(8,128)} %get-tuple-element.259, f32[2048]{0:T(1024)S(1)} %bitcast.110, s32[2048]{0:T(1024)S(1)} %get-tuple-element.292, s32[1024]{0:T(1024)S(1)} %dynamic_slice.32, f32[1,88,2048]{2,1,0:T(8,128)S(1)} %get-tuple-element.278, f32[2048]{0:T(1024)S(1)} %bitcast.117, ...), kind=kOutput, calls=%fused_computation.12.clone.1 | convolution fusion | flops 380125184 | bytes 10039305 | tf_op jit(solution)/shard_map/while/body/eval_jaxpr/hqk,hdk->hdq/dot_general | solution.py:73
  164.3 5.6 %fusion.45 = (f32[2048]{0:T(1024)S(1)}, f32[1024,2048]{1,0:T(8,128)}) fusion(s32[2048]{0:T(1024)S(1)} %get-tuple-element.292, s32[1024]{0:T(1024)S(1)} %dynamic_slice.32, bf16[1,88,2048]{2,1,0:T(8,128)(2,1)S(1)} %get-tuple-element.295, bf16[2,88,16384]{2,1,0:T(8,128)(2,1)} %get-tuple-element.294, s32[]{:T(128)S(6)} %select_n.132), kind=kOutput, calls=%fused_computation.5.clone.1 | convolution fusion | flops 377485312 | bytes 8949764 | tf_op jit(solution)/shard_map/while/body/eval_jaxpr/hdq,hdk->hqk/dot_general | solution.py:65
  169.9 4.6 fusion.47
  174.5 5.4 %fusion.49 = f32[1,88,2048]{2,1,0:T(8,128)S(1)} fusion(f32[1024,2048]{1,0:T(8,128)} %get-tuple-element.259, f32[2048]{0:T(1024)S(1)} %bitcast.110, s32[2048]{0:T(1024)S(1)} %get-tuple-element.292, s32[1024]{0:T(1024)S(1)} %dynamic_slice.32, f32[1,88,2048]{2,1,0:T(8,128)S(1)} %get-tuple-element.278, f32[2048]{0:T(1024)S(1)} %bitcast.117, ...), kind=kOutput, calls=%fused_computation.12.clone.1 | convolution fusion | flops 380125184 | bytes 10039305 | tf_op jit(solution)/shard_map/while/body/eval_jaxpr/hqk,hdk->hdq/dot_general | solution.py:73
  180.0 5.6 %fusion.45 = (f32[2048]{0:T(1024)S(1)}, f32[1024,2048]{1,0:T(8,128)}) fusion(s32[2048]{0:T(1024)S(1)} %get-tuple-element.292, s32[1024]{0:T(1024)S(1)} %dynamic_slice.32, bf16[1,88,2048]{2,1,0:T(8,128)(2,1)S(1)} %get-tuple-element.295, bf16[2,88,16384]{2,1,0:T(8,128)(2,1)} %get-tuple-element.294, s32[]{:T(128)S(6)} %select_n.132), kind=kOutput, calls=%fused_computation.5.clone.1 | convolution fusion | flops 377485312 | bytes 8949764 | tf_op jit(solution)/shard_map/while/body/eval_jaxpr/hdq,hdk->hqk/dot_general | solution.py:65
  185.6 4.7 fusion.47
  190.4 5.4 %fusion.49 = f32[1,88,2048]{2,1,0:T(8,128)S(1)} fusion(f32[1024,2048]{1,0:T(8,128)} %get-tuple-element.259, f32[2048]{0:T(1024)S(1)} %bitcast.110, s32[2048]{0:T(1024)S(1)} %get-tuple-element.292, s32[1024]{0:T(1024)S(1)} %dynamic_slice.32, f32[1,88,2048]{2,1,0:T(8,128)S(1)} %get-tuple-element.278, f32[2048]{0:T(1024)S(1)} %bitcast.117, ...), kind=kOutput, calls=%fused_computation.12.clone.1 | convolution fusion | flops 380125184 | bytes 10039305 | tf_op jit(solution)/shard_map/while/body/eval_jaxpr/hqk,hdk->hdq/dot_general | solution.py:73
  195.8 5.6 %fusion.45 = (f32[2048]{0:T(1024)S(1)}, f32[1024,2048]{1,0:T(8,128)}) fusion(s32[2048]{0:T(1024)S(1)} %get-tuple-element.292, s32[1024]{0:T(1024)S(1)} %dynamic_slice.32, bf16[1,88,2048]{2,1,0:T(8,128)(2,1)S(1)} %get-tuple-element.295, bf16[2,88,16384]{2,1,0:T(8,128)(2,1)} %get-tuple-element.294, s32[]{:T(128)S(6)} %select_n.132), kind=kOutput, calls=%fused_computation.5.clone.1 | convolution fusion | flops 377485312 | bytes 8949764 | tf_op jit(solution)/shard_map/while/body/eval_jaxpr/hdq,hdk->hqk/dot_general | solution.py:65
  201.4 4.6 fusion.47
  206.0 5.9 %fusion.49 = f32[1,88,2048]{2,1,0:T(8,128)S(1)} fusion(f32[1024,2048]{1,0:T(8,128)} %get-tuple-element.259, f32[2048]{0:T(1024)S(1)} %bitcast.110, s32[2048]{0:T(1024)S(1)} %get-tuple-element.292, s32[1024]{0:T(1024)S(1)} %dynamic_slice.32, f32[1,88,2048]{2,1,0:T(8,128)S(1)} %get-tuple-element.278, f32[2048]{0:T(1024)S(1)} %bitcast.117, ...), kind=kOutput, calls=%fused_computation.12.clone.1 | convolution fusion | flops 380125184 | bytes 10039305 | tf_op jit(solution)/shard_map/while/body/eval_jaxpr/hqk,hdk->hdq/dot_general | solution.py:73
  212.0 5.6 %fusion.45 = (f32[2048]{0:T(1024)S(1)}, f32[1024,2048]{1,0:T(8,128)}) fusion(s32[2048]{0:T(1024)S(1)} %get-tuple-element.292, s32[1024]{0:T(1024)S(1)} %dynamic_slice.32, bf16[1,88,2048]{2,1,0:T(8,128)(2,1)S(1)} %get-tuple-element.295, bf16[2,88,16384]{2,1,0:T(8,128)(2,1)} %get-tuple-element.294, s32[]{:T(128)S(6)} %select_n.132), kind=kOutput, calls=%fused_computation.5.clone.1 | convolution fusion | flops 377485312 | bytes 8949764 | tf_op jit(solution)/shard_map/while/body/eval_jaxpr/hdq,hdk->hqk/dot_general | solution.py:65
  217.5 4.7 fusion.47
  222.3 5.4 %fusion.49 = f32[1,88,2048]{2,1,0:T(8,128)S(1)} fusion(f32[1024,2048]{1,0:T(8,128)} %get-tuple-element.259, f32[2048]{0:T(1024)S(1)} %bitcast.110, s32[2048]{0:T(1024)S(1)} %get-tuple-element.292, s32[1024]{0:T(1024)S(1)} %dynamic_slice.32, f32[1,88,2048]{2,1,0:T(8,128)S(1)} %get-tuple-element.278, f32[2048]{0:T(1024)S(1)} %bitcast.117, ...), kind=kOutput, calls=%fused_computation.12.clone.1 | convolution fusion | flops 380125184 | bytes 10039305 | tf_op jit(solution)/shard_map/while/body/eval_jaxpr/hqk,hdk->hdq/dot_general | solution.py:73
  227.8 5.6 %fusion.45 = (f32[2048]{0:T(1024)S(1)}, f32[1024,2048]{1,0:T(8,128)}) fusion(s32[2048]{0:T(1024)S(1)} %get-tuple-element.292, s32[1024]{0:T(1024)S(1)} %dynamic_slice.32, bf16[1,88,2048]{2,1,0:T(8,128)(2,1)S(1)} %get-tuple-element.295, bf16[2,88,16384]{2,1,0:T(8,128)(2,1)} %get-tuple-element.294, s32[]{:T(128)S(6)} %select_n.132), kind=kOutput, calls=%fused_computation.5.clone.1 | convolution fusion | flops 377485312 | bytes 8949764 | tf_op jit(solution)/shard_map/while/body/eval_jaxpr/hdq,hdk->hqk/dot_general | solution.py:65
  233.4 5.9 %fusion.47 = f32[2048]{0:T(1024)S(1)} fusion(f32[1024,2048]{1,0:T(8,128)} %get-tuple-element.259, f32[2048]{0:T(1024)S(1)} %bitcast.109, s32[2048]{0:T(1024)S(1)} %get-tuple-element.292, s32[1024]{0:T(1024)S(1)} %dynamic_slice.32), kind=kLoop, calls=%fused_computation.9.clone.1 | loop fusion | flops 10483712 | bytes 8417280 | tf_op jit(solution)/shard_map/while/body/eval_jaxpr/reduce_sum | solution.py:72
  239.3 5.4 %fusion.49 = f32[1,88,2048]{2,1,0:T(8,128)S(1)} fusion(f32[1024,2048]{1,0:T(8,128)} %get-tuple-element.259, f32[2048]{0:T(1024)S(1)} %bitcast.110, s32[2048]{0:T(1024)S(1)} %get-tuple-element.292, s32[1024]{0:T(1024)S(1)} %dynamic_slice.32, f32[1,88,2048]{2,1,0:T(8,128)S(1)} %get-tuple-element.278, f32[2048]{0:T(1024)S(1)} %bitcast.117, ...), kind=kOutput, calls=%fused_computation.12.clone.1 | convolution fusion | flops 380125184 | bytes 10039305 | tf_op jit(solution)/shard_map/while/body/eval_jaxpr/hqk,hdk->hdq/dot_general | solution.py:73
  244.8 5.6 %fusion.45 = (f32[2048]{0:T(1024)S(1)}, f32[1024,2048]{1,0:T(8,128)}) fusion(s32[2048]{0:T(1024)S(1)} %get-tuple-element.292, s32[1024]{0:T(1024)S(1)} %dynamic_slice.32, bf16[1,88,2048]{2,1,0:T(8,128)(2,1)S(1)} %get-tuple-element.295, bf16[2,88,16384]{2,1,0:T(8,128)(2,1)} %get-tuple-element.294, s32[]{:T(128)S(6)} %select_n.132), kind=kOutput, calls=%fused_computation.5.clone.1 | convolution fusion | flops 377485312 | bytes 8949764 | tf_op jit(solution)/shard_map/while/body/eval_jaxpr/hdq,hdk->hqk/dot_general | solution.py:65
  250.4 4.8 fusion.47
  255.2 5.7 %fusion.49 = f32[1,88,2048]{2,1,0:T(8,128)S(1)} fusion(f32[1024,2048]{1,0:T(8,128)} %get-tuple-element.259, f32[2048]{0:T(1024)S(1)} %bitcast.110, s32[2048]{0:T(1024)S(1)} %get-tuple-element.292, s32[1024]{0:T(1024)S(1)} %dynamic_slice.32, f32[1,88,2048]{2,1,0:T(8,128)S(1)} %get-tuple-element.278, f32[2048]{0:T(1024)S(1)} %bitcast.117, ...), kind=kOutput, calls=%fused_computation.12.clone.1 | convolution fusion | flops 380125184 | bytes 10039305 | tf_op jit(solution)/shard_map/while/body/eval_jaxpr/hqk,hdk->hdq/dot_general | solution.py:73
  261.0 5.6 %fusion.45 = (f32[2048]{0:T(1024)S(1)}, f32[1024,2048]{1,0:T(8,128)}) fusion(s32[2048]{0:T(1024)S(1)} %get-tuple-element.292, s32[1024]{0:T(1024)S(1)} %dynamic_slice.32, bf16[1,88,2048]{2,1,0:T(8,128)(2,1)S(1)} %get-tuple-element.295, bf16[2,88,16384]{2,1,0:T(8,128)(2,1)} %get-tuple-element.294, s32[]{:T(128)S(6)} %select_n.132), kind=kOutput, calls=%fused_computation.5.clone.1 | convolution fusion | flops 377485312 | bytes 8949764 | tf_op jit(solution)/shard_map/while/body/eval_jaxpr/hdq,hdk->hqk/dot_general | solution.py:65
  266.6 4.8 fusion.47
  271.4 5.7 %fusion.49 = f32[1,88,2048]{2,1,0:T(8,128)S(1)} fusion(f32[1024,2048]{1,0:T(8,128)} %get-tuple-element.259, f32[2048]{0:T(1024)S(1)} %bitcast.110, s32[2048]{0:T(1024)S(1)} %get-tuple-element.292, s32[1024]{0:T(1024)S(1)} %dynamic_slice.32, f32[1,88,2048]{2,1,0:T(8,128)S(1)} %get-tuple-element.278, f32[2048]{0:T(1024)S(1)} %bitcast.117, ...), kind=kOutput, calls=%fused_computation.12.clone.1 | convolution fusion | flops 380125184 | bytes 10039305 | tf_op jit(solution)/shard_map/while/body/eval_jaxpr/hqk,hdk->hdq/dot_general | solution.py:73
  277.1 5.6 %fusion.45 = (f32[2048]{0:T(1024)S(1)}, f32[1024,2048]{1,0:T(8,128)}) fusion(s32[2048]{0:T(1024)S(1)} %get-tuple-element.292, s32[1024]{0:T(1024)S(1)} %dynamic_slice.32, bf16[1,88,2048]{2,1,0:T(8,128)(2,1)S(1)} %get-tuple-element.295, bf16[2,88,16384]{2,1,0:T(8,128)(2,1)} %get-tuple-element.294, s32[]{:T(128)S(6)} %select_n.132), kind=kOutput, calls=%fused_computation.5.clone.1 | convolution fusion | flops 377485312 | bytes 8949764 | tf_op jit(solution)/shard_map/while/body/eval_jaxpr/hdq,hdk->hqk/dot_general | solution.py:65
  282.7 4.7 fusion.47
  287.4 5.4 %fusion.49 = f32[1,88,2048]{2,1,0:T(8,128)S(1)} fusion(f32[1024,2048]{1,0:T(8,128)} %get-tuple-element.259, f32[2048]{0:T(1024)S(1)} %bitcast.110, s32[2048]{0:T(1024)S(1)} %get-tuple-element.292, s32[1024]{0:T(1024)S(1)} %dynamic_slice.32, f32[1,88,2048]{2,1,0:T(8,128)S(1)} %get-tuple-element.278, f32[2048]{0:T(1024)S(1)} %bitcast.117, ...), kind=kOutput, calls=%fused_computation.12.clone.1 | convolution fusion | flops 380125184 | bytes 10039305 | tf_op jit(solution)/shard_map/while/body/eval_jaxpr/hqk,hdk->hdq/dot_general | solution.py:73
  292.9 5.6 %fusion.45 = (f32[2048]{0:T(1024)S(1)}, f32[1024,2048]{1,0:T(8,128)}) fusion(s32[2048]{0:T(1024)S(1)} %get-tuple-element.292, s32[1024]{0:T(1024)S(1)} %dynamic_slice.32, bf16[1,88,2048]{2,1,0:T(8,128)(2,1)S(1)} %get-tuple-element.295, bf16[2,88,16384]{2,1,0:T(8,128)(2,1)} %get-tuple-element.294, s32[]{:T(128)S(6)} %select_n.132), kind=kOutput, calls=%fused_computation.5.clone.1 | convolution fusion | flops 377485312 | bytes 8949764 | tf_op jit(solution)/shard_map/while/body/eval_jaxpr/hdq,hdk->hqk/dot_general | solution.py:65
  298.5 4.6 fusion.47
  303.1 5.4 %fusion.49 = f32[1,88,2048]{2,1,0:T(8,128)S(1)} fusion(f32[1024,2048]{1,0:T(8,128)} %get-tuple-element.259, f32[2048]{0:T(1024)S(1)} %bitcast.110, s32[2048]{0:T(1024)S(1)} %get-tuple-element.292, s32[1024]{0:T(1024)S(1)} %dynamic_slice.32, f32[1,88,2048]{2,1,0:T(8,128)S(1)} %get-tuple-element.278, f32[2048]{0:T(1024)S(1)} %bitcast.117, ...), kind=kOutput, calls=%fused_computation.12.clone.1 | convolution fusion | flops 380125184 | bytes 10039305 | tf_op jit(solution)/shard_map/while/body/eval_jaxpr/hqk,hdk->hdq/dot_general | solution.py:73
  308.6 5.6 %fusion.45 = (f32[2048]{0:T(1024)S(1)}, f32[1024,2048]{1,0:T(8,128)}) fusion(s32[2048]{0:T(1024)S(1)} %get-tuple-element.292, s32[1024]{0:T(1024)S(1)} %dynamic_slice.32, bf16[1,88,2048]{2,1,0:T(8,128)(2,1)S(1)} %get-tuple-element.295, bf16[2,88,16384]{2,1,0:T(8,128)(2,1)} %get-tuple-element.294, s32[]{:T(128)S(6)} %select_n.132), kind=kOutput, calls=%fused_computation.5.clone.1 | convolution fusion | flops 377485312 | bytes 8949764 | tf_op jit(solution)/shard_map/while/body/eval_jaxpr/hdq,hdk->hqk/dot_general | solution.py:65
  314.1 4.6 fusion.47
  318.8 5.4 %fusion.49 = f32[1,88,2048]{2,1,0:T(8,128)S(1)} fusion(f32[1024,2048]{1,0:T(8,128)} %get-tuple-element.259, f32[2048]{0:T(1024)S(1)} %bitcast.110, s32[2048]{0:T(1024)S(1)} %get-tuple-element.292, s32[1024]{0:T(1024)S(1)} %dynamic_slice.32, f32[1,88,2048]{2,1,0:T(8,128)S(1)} %get-tuple-element.278, f32[2048]{0:T(1024)S(1)} %bitcast.117, ...), kind=kOutput, calls=%fused_computation.12.clone.1 | convolution fusion | flops 380125184 | bytes 10039305 | tf_op jit(solution)/shard_map/while/body/eval_jaxpr/hqk,hdk->hdq/dot_general | solution.py:73
  324.2 5.6 %fusion.45 = (f32[2048]{0:T(1024)S(1)}, f32[1024,2048]{1,0:T(8,128)}) fusion(s32[2048]{0:T(1024)S(1)} %get-tuple-element.292, s32[1024]{0:T(1024)S(1)} %dynamic_slice.32, bf16[1,88,2048]{2,1,0:T(8,128)(2,1)S(1)} %get-tuple-element.295, bf16[2,88,16384]{2,1,0:T(8,128)(2,1)} %get-tuple-element.294, s32[]{:T(128)S(6)} %select_n.132), kind=kOutput, calls=%fused_computation.5.clone.1 | convolution fusion | flops 377485312 | bytes 8949764 | tf_op jit(solution)/shard_map/while/body/eval_jaxpr/hdq,hdk->hqk/dot_general | solution.py:65
  329.8 4.6 fusion.47
  334.4 5.4 %fusion.49 = f32[1,88,2048]{2,1,0:T(8,128)S(1)} fusion(f32[1024,2048]{1,0:T(8,128)} %get-tuple-element.259, f32[2048]{0:T(1024)S(1)} %bitcast.110, s32[2048]{0:T(1024)S(1)} %get-tuple-element.292, s32[1024]{0:T(1024)S(1)} %dynamic_slice.32, f32[1,88,2048]{2,1,0:T(8,128)S(1)} %get-tuple-element.278, f32[2048]{0:T(1024)S(1)} %bitcast.117, ...), kind=kOutput, calls=%fused_computation.12.clone.1 | convolution fusion | flops 380125184 | bytes 10039305 | tf_op jit(solution)/shard_map/while/body/eval_jaxpr/hqk,hdk->hdq/dot_general | solution.py:73
  339.9 5.6 %fusion.45 = (f32[2048]{0:T(1024)S(1)}, f32[1024,2048]{1,0:T(8,128)}) fusion(s32[2048]{0:T(1024)S(1)} %get-tuple-element.292, s32[1024]{0:T(1024)S(1)} %dynamic_slice.32, bf16[1,88,2048]{2,1,0:T(8,128)(2,1)S(1)} %get-tuple-element.295, bf16[2,88,16384]{2,1,0:T(8,128)(2,1)} %get-tuple-element.294, s32[]{:T(128)S(6)} %select_n.132), kind=kOutput, calls=%fused_computation.5.clone.1 | convolution fusion | flops 377485312 | bytes 8949764 | tf_op jit(solution)/shard_map/while/body/eval_jaxpr/hdq,hdk->hqk/dot_general | solution.py:65
  345.5 4.6 fusion.47
  350.1 5.4 %fusion.49 = f32[1,88,2048]{2,1,0:T(8,128)S(1)} fusion(f32[1024,2048]{1,0:T(8,128)} %get-tuple-element.259, f32[2048]{0:T(1024)S(1)} %bitcast.110, s32[2048]{0:T(1024)S(1)} %get-tuple-element.292, s32[1024]{0:T(1024)S(1)} %dynamic_slice.32, f32[1,88,2048]{2,1,0:T(8,128)S(1)} %get-tuple-element.278, f32[2048]{0:T(1024)S(1)} %bitcast.117, ...), kind=kOutput, calls=%fused_computation.12.clone.1 | convolution fusion | flops 380125184 | bytes 10039305 | tf_op jit(solution)/shard_map/while/body/eval_jaxpr/hqk,hdk->hdq/dot_general | solution.py:73
  355.6 5.6 %fusion.45 = (f32[2048]{0:T(1024)S(1)}, f32[1024,2048]{1,0:T(8,128)}) fusion(s32[2048]{0:T(1024)S(1)} %get-tuple-element.292, s32[1024]{0:T(1024)S(1)} %dynamic_slice.32, bf16[1,88,2048]{2,1,0:T(8,128)(2,1)S(1)} %get-tuple-element.295, bf16[2,88,16384]{2,1,0:T(8,128)(2,1)} %get-tuple-element.294, s32[]{:T(128)S(6)} %select_n.132), kind=kOutput, calls=%fused_computation.5.clone.1 | convolution fusion | flops 377485312 | bytes 8949764 | tf_op jit(solution)/shard_map/while/body/eval_jaxpr/hdq,hdk->hqk/dot_general | solution.py:65
  361.1 4.6 fusion.47
  365.8 5.4 %fusion.49 = f32[1,88,2048]{2,1,0:T(8,128)S(1)} fusion(f32[1024,2048]{1,0:T(8,128)} %get-tuple-element.259, f32[2048]{0:T(1024)S(1)} %bitcast.110, s32[2048]{0:T(1024)S(1)} %get-tuple-element.292, s32[1024]{0:T(1024)S(1)} %dynamic_slice.32, f32[1,88,2048]{2,1,0:T(8,128)S(1)} %get-tuple-element.278, f32[2048]{0:T(1024)S(1)} %bitcast.117, ...), kind=kOutput, calls=%fused_computation.12.clone.1 | convolution fusion | flops 380125184 | bytes 10039305 | tf_op jit(solution)/shard_map/while/body/eval_jaxpr/hqk,hdk->hdq/dot_general | solution.py:73
  371.2 5.6 %fusion.45 = (f32[2048]{0:T(1024)S(1)}, f32[1024,2048]{1,0:T(8,128)}) fusion(s32[2048]{0:T(1024)S(1)} %get-tuple-element.292, s32[1024]{0:T(1024)S(1)} %dynamic_slice.32, bf16[1,88,2048]{2,1,0:T(8,128)(2,1)S(1)} %get-tuple-element.295, bf16[2,88,16384]{2,1,0:T(8,128)(2,1)} %get-tuple-element.294, s32[]{:T(128)S(6)} %select_n.132), kind=kOutput, calls=%fused_computation.5.clone.1 | convolution fusion | flops 377485312 | bytes 8949764 | tf_op jit(solution)/shard_map/while/body/eval_jaxpr/hdq,hdk->hqk/dot_general | solution.py:65
  376.8 4.6 fusion.47
  381.4 5.4 %fusion.49 = f32[1,88,2048]{2,1,0:T(8,128)S(1)} fusion(f32[1024,2048]{1,0:T(8,128)} %get-tuple-element.259, f32[2048]{0:T(1024)S(1)} %bitcast.110, s32[2048]{0:T(1024)S(1)} %get-tuple-element.292, s32[1024]{0:T(1024)S(1)} %dynamic_slice.32, f32[1,88,2048]{2,1,0:T(8,128)S(1)} %get-tuple-element.278, f32[2048]{0:T(1024)S(1)} %bitcast.117, ...), kind=kOutput, calls=%fused_computation.12.clone.1 | convolution fusion | flops 380125184 | bytes 10039305 | tf_op jit(solution)/shard_map/while/body/eval_jaxpr/hqk,hdk->hdq/dot_general | solution.py:73
  386.9 5.6 %fusion.45 = (f32[2048]{0:T(1024)S(1)}, f32[1024,2048]{1,0:T(8,128)}) fusion(s32[2048]{0:T(1024)S(1)} %get-tuple-element.292, s32[1024]{0:T(1024)S(1)} %dynamic_slice.32, bf16[1,88,2048]{2,1,0:T(8,128)(2,1)S(1)} %get-tuple-element.295, bf16[2,88,16384]{2,1,0:T(8,128)(2,1)} %get-tuple-element.294, s32[]{:T(128)S(6)} %select_n.132), kind=kOutput, calls=%fused_computation.5.clone.1 | convolution fusion | flops 377485312 | bytes 8949764 | tf_op jit(solution)/shard_map/while/body/eval_jaxpr/hdq,hdk->hqk/dot_general | solution.py:65
  392.5 4.6 fusion.47
  397.1 5.4 %fusion.49 = f32[1,88,2048]{2,1,0:T(8,128)S(1)} fusion(f32[1024,2048]{1,0:T(8,128)} %get-tuple-element.259, f32[2048]{0:T(1024)S(1)} %bitcast.110, s32[2048]{0:T(1024)S(1)} %get-tuple-element.292, s32[1024]{0:T(1024)S(1)} %dynamic_slice.32, f32[1,88,2048]{2,1,0:T(8,128)S(1)} %get-tuple-element.278, f32[2048]{0:T(1024)S(1)} %bitcast.117, ...), kind=kOutput, calls=%fused_computation.12.clone.1 | convolution fusion | flops 380125184 | bytes 10039305 | tf_op jit(solution)/shard_map/while/body/eval_jaxpr/hqk,hdk->hdq/dot_general | solution.py:73
  403.5 6.1 %all-to-all-start = ((bf16[88,16,128]{2,0,1:T(8,128)(2,1)}), bf16[88,16,128]{2,0,1:T(8,128)(2,1)S(1)}, u32[]{:S(2)}, u32[]{:S(2)}) async-start(bf16[88,16,128]{2,0,1:T(8,128)(2,1)} %copy.32), calls=%async_computation | async-start | bytes 720896 | tf_op jit(solution)/shard_map/all_to_all | solution.py:102
  409.7 7.7 %convert_element_type.50 = f32[1408,2048]{0,1:T(8,128)} convert(bf16[1408,2048]{0,1:T(8,128)(2,1)} %copy.28) | non-fusion elementwise | flops 2883584 | bytes 17301504 | tf_op jit(solution)/shard_map/convert_element_type | solution.py:33
  419.5 3.2 fusion.31
  423.1 8.8 %fusion.23 = bf16[32,1408]{1,0:T(8,128)(2,1)} fusion(bf16[4,1408,1408]{2,1,0:T(8,128)(2,1)} %all-gather.12.cloned.1.call-done, bf16[1408,32,4]{0,2,1:T(4,128)(2,1)S(1)} %reshape.212), kind=kOutput, calls=%fused_computation.36 | convolution fusion | flops 507555840 | bytes 16310272 | tf_op jit(solution)/shard_map/fgi,ifd->gd/dot_general | solution.py:118
  433.3 41.2 %all-gather.14.cloned.1.call-done = bf16[512,1408]{1,0:T(8,128)(2,1)} async-done(((bf16[32,1408]{1,0:T(8,128)(2,1)}), bf16[512,1408]{1,0:T(8,128)(2,1)}) %all-gather.14.cloned.1.call-update) | async-done | bytes 1441808 | tf_op jit(solution)/shard_map/all_gather | solution.py:119
  474.5 2.5 gather_fusion.1
  (116 shorter events, 16.9 us)
Async XLA Ops:
  6.5 86.1 %copy-start = (bf16[2,88,1408]{2,1,0:T(8,128)(2,1)S(1)}, bf16[2,88,1408]{2,1,0:T(8,128)(2,1)}, u32[]{:S(2)}) copy-start(bf16[2,88,1408]{2,1,0:T(8,128)(2,1)} %param.16) | copy-start | bytes 1486852
  6.5 64.2 %all-gather.6.cloned.1.call-start = ((), (), s32[]{:S(2)}) async-start(), calls=%async_computation.1 | async-start | bytes 6127616 | tf_op jit(solution)/shard_map/all_gather | solution.py:31
  7.3 134.4 %all-gather.8.cloned.1.call-start = ((), (), s32[]{:S(2)}) async-start(), calls=%async_computation.2 | async-start | bytes 6782976 | tf_op jit(solution)/shard_map/all_gather | solution.py:56
  79.1 4.5 copy-start.2
  87.6 15.2 %copy-start.4 = (bf16[88,1408]{1,0:T(8,128)(2,1)S(1)}, bf16[88,1408]{1,0:T(8,128)(2,1)}, u32[]{:S(2)}) copy-start(bf16[88,1408]{1,0:T(8,128)(2,1)} %param.15) | copy-start | bytes 743428
  101.8 315.6 %all-gather.10.cloned.1.call-start = ((), (), s32[]{:S(2)}) async-start(), calls=%async_computation.3 | async-start | bytes 4212736 | tf_op jit(solution)/shard_map/all_gather | solution.py:32
  102.5 320.5 %all-gather.12.cloned.1.call-start = ((), (), s32[]{:S(2)}) async-start(), calls=%async_computation.4 | async-start | bytes 16850944 | tf_op jit(solution)/shard_map/all_gather | solution.py:116
  102.8 45.7 %copy-start.3 = (s32[2048]{0:T(1024)S(1)}, s32[2048]{0:T(1024)}, u32[]{:S(2)}) copy-start(s32[2048]{0:T(1024)} %param.19) | copy-start | bytes 24580
  148.5 261.2 %copy-start.5 = (bf16[1408]{0:T(1024)(128)(2,1)S(1)}, bf16[1408]{0:T(1024)(128)(2,1)}, u32[]{:S(2)}) copy-start(bf16[1408]{0:T(1024)(128)(2,1)} %param.21) | copy-start | bytes 8452
  403.5 16.0 %all-to-all-start = ((bf16[88,16,128]{2,0,1:T(8,128)(2,1)}), bf16[88,16,128]{2,0,1:T(8,128)(2,1)S(1)}, u32[]{:S(2)}, u32[]{:S(2)}) async-start(bf16[88,16,128]{2,0,1:T(8,128)(2,1)} %copy.32), calls=%async_computation | async-start | bytes 720896 | tf_op jit(solution)/shard_map/all_to_all | solution.py:102
  409.6 64.9 %all-gather.14.cloned.1.call-start = ((), (), s32[]{:S(2)}) async-start(), calls=%async_computation.5 | async-start | bytes 1531904 | tf_op jit(solution)/shard_map/all_gather | solution.py:119
  422.9 54.9 %copy-start.1 = (bf16[2,88,1408]{2,1,0:T(8,128)(2,1)S(1)}, bf16[2,88,1408]{2,1,0:T(8,128)(2,1)}, u32[]{:S(2)}) copy-start(bf16[2,88,1408]{2,1,0:T(8,128)(2,1)} %param.16) | copy-start | bytes 1486852
Sparse Core Ops, SparseCore 0:
  9.5 61.1 all-gather.5
  101.9 39.7 all-gather.7
  143.8 50.4 all-gather.9
  196.4 106.0 all-gather.11
  432.0 42.4 all-gather.13
where the time goes:
time: 486 us; the launch traced here: 484 us
  matrix products  194 us (40%)
  waiting for transfers between devices  137 us (28%)
  other arithmetic  99.7 us (21%)
  local copies, waits for them, and re-layouts  33 us (7%)
  between operations  13.4 us (3%)
  starting transfers between devices  6.4 us (1%)
    dot_general x16, matrix products, take_block(): jnp.einsum('hdq,hdk->hqk', query_heads, key_block, preferred_element_type...  89.1 us
    dot_general x16, matrix products, take_block(): jnp.einsum('hqk,hdk->hdq', weights_exp.astype(jnp.bfloat16), value_block,...  87.5 us
    reduce_sum x16, other arithmetic, take_block(): running_sum = running_sum * factor + jnp.sum(weights_exp, axis=2)  75.4 us
    all_gather x1, waiting for transfers between devices, on_device(): full_rows = lax.all_gather(hidden, 'col', axis=0, tiled=True)  58.2 us
    all_gather x1, waiting for transfers between devices, on_device(): lax.all_gather(merged_here.astype(jnp.bfloat16), 'col', axis=0, tiled=True)  41.2 us
    all_gather x1, waiting for transfers between devices, on_device(): pair_all = lax.all_gather(pair_local, 'row', axis=1, tiled=True)  34.2 us
  transfers between devices with their start and end apart: 6, of which 4 were waited for; matrix products, arithmetic and copies ran while one was open for 58% of the time, Pallas kernels for 0%

commit v1 on v0

--- a/solution.py
+++ b/solution.py
@@ -28,8 +28,13 @@
     heads_here = local_width // HD
     score_scale = HD ** (-0.5)
     col_index = lax.axis_index("col")
-    full_rows = lax.all_gather(hidden, "col", axis=0, tiled=True)
-    out_weight = lax.all_gather(w_out, "col", axis=0, tiled=True)
+
+    def weights_link(xx, inner_x):
+        x_next = jnp.concatenate([xx, inner_x], axis=1)
+        side_arr = lax.all_gather(x_next, "col", axis=0, tiled=True)
+        return jnp.split(side_arr, [xx.shape[1]], axis=1)
+
+    full_rows, out_weight = weights_link(hidden, w_out)
     full_float = full_rows.astype(jnp.float32)
     in_mean = jnp.sum(full_float, axis=0, keepdims=True) / model_width
     in_square = jnp.sum(full_float * full_float, axis=0, keepdims=True) / model_width

time: 486 us -> 509 us (1.047)
  waiting for transfers between devices: 137 us -> 154 us
  local copies, waits for them, and re-layouts: 33 us -> 39 us
    all_gather x2 -> x1, waiting for transfers between devices: 58.3 us -> 75.2 us  [weights_link(): side_arr = lax.all_gather(x_next, 'col', axis=0, tiled=True)]
    unnamed x14 -> x15, local copies, waits for them, and re-layouts: 2.47 us -> 10.9 us
    all_gather x1 -> x0, local copies, waits for them, and re-layouts: 8.33 us -> none  [on_device(): full_rows = lax.all_gather(hidden, 'col', axis=0, tiled=True)]
    split x0 -> x1, local copies, waits for them, and re-layouts: none -> 6.03 us  [weights_link(): return jnp.split(side_arr, [xx.shape[1]], axis=1)]
  transfers between devices with their start and end apart: 6 -> 5, of which waited for: 4 -> 4; matrix products, arithmetic and copies ran while one was open for 58% -> 55% of each run, Pallas kernels for 0% -> 0%
where the time goes in v1:
time: 509 us; the launch traced here: 508 us
  matrix products  194 us (38%)
  waiting for transfers between devices  154 us (30%)
  other arithmetic  100 us (20%)
  local copies, waits for them, and re-layouts  39 us (8%)
  between operations  13.4 us (3%)
  starting transfers between devices  6.72 us (1%)
    dot_general x16, matrix products, take_block(): jnp.einsum('hdq,hdk->hqk', query_heads, key_block, preferred_element_type...  89.2 us
    dot_general x16, matrix products, take_block(): jnp.einsum('hqk,hdk->hdq', weights_exp.astype(jnp.bfloat16), value_block,...  87.3 us
    all_gather x1, waiting for transfers between devices, weights_link(): side_arr = lax.all_gather(x_next, 'col', axis=0, tiled=True)  75.2 us
    reduce_sum x16, other arithmetic, take_block(): running_sum = running_sum * factor + jnp.sum(weights_exp, axis=2)  74.2 us
    all_gather x1, waiting for transfers between devices, on_device(): lax.all_gather(merged_here.astype(jnp.bfloat16), 'col', axis=0, tiled=True)  41.4 us
    all_gather x1, waiting for transfers between devices, on_device(): pair_all = lax.all_gather(pair_local, 'row', axis=1, tiled=True)  35 us
    unnamed x15, local copies, waits for them, and re-layouts  10.9 us
  transfers between devices with their start and end apart: 5, of which 4 were waited for; matrix products, arithmetic and copies ran while one was open for 55% of the time, Pallas kernels for 0%

profile of v1, /device:TPU:0, one launch (start us, length us, event | category | flops | bytes accessed | tf_op | source)
XLA Modules:
  0.0 507.6 jit_solution(5871661828501224413)
XLA Ops:
  13.8 75.2 %all-gather.5.cloned.1.call-done = bf16[1408,3456]{1,0:T(8,128)(2,1)} async-done(((bf16[88,3456]{1,0:T(8,128)(2,1)}), bf16[1408,3456]{1,0:T(8,128)(2,1)}) %all-gather.5.cloned.1.call-update) | async-done | bytes 9732112 | tf_op jit(solution)/shard_map/all_gather | solution.py:34
  89.0 6.0 %split.8 = bf16[1408,2048]{1,0:T(8,128)(2,1)} slice(bf16[1408,3456]{1,0:T(8,128)(2,1)} %all-gather.5.cloned.1.call-done), slice={[0:1408], [0:2048]} | slice | bytes 11534336 | tf_op jit(solution)/shard_map/split | solution.py:35
  95.1 8.4 %copy.37 = bf16[1408,2048]{0,1:T(8,128)(2,1)} copy(bf16[1408,2048]{1,0:T(8,128)(2,1)} %split.8) | data formatting | bytes 11534336
  103.5 4.5 convert_reduce_fusion
  108.0 3.9 multiply_convert_fusion
  111.9 5.0 gather_fusion
  117.5 6.9 %scatter_fusion = bf16[2,88,2048]{1,0,2:T(2,128)(2,1)S(1)} fusion(bf16[2,88,2048]{1,0,2:T(2,128)(2,1)S(1)} %copy.33, s32[200]{0:T(256)S(1)} %bitcast.117, bf16[200,2,88]{2,1,0:T(2,128)(2,1)S(1)} %bitcast.109), kind=kCustom, calls=%fused_computation.2 | custom fusion | bytes 212000 | tf_op jit(solution)/shard_map/scatter | solution.py:55
  126.4 4.7 fusion.26
  131.1 35.0 %all-gather.7.cloned.1.call-done = bf16[177,16384]{1,0:T(8,128)(2,1)} async-done(((bf16[177,2048]{1,0:T(8,128)(2,1)}), bf16[177,16384]{1,0:T(8,128)(2,1)}) %all-gather.7.cloned.1.call-update) | async-done | bytes 5799952 | tf_op jit(solution)/shard_map/all_gather | solution.py:61
  166.0 5.7 %slice.29 = bf16[176,16384]{1,0:T(8,128)(2,1)} slice(bf16[177,16384]{1,0:T(8,128)(2,1)} %all-gather.7.cloned.1.call-done), slice={[0:176], [0:16384]} | slice | bytes 11534336 | tf_op jit(solution)/shard_map/slice | solution.py:62
  172.8 252.6 %while.18 = (s32[]{:T(128)}, f32[1,2048]{1,0:T(1,128)S(1)}, f32[1,2048]{1,0:T(1,128)S(1)}, f32[1,88,2048]{2,1,0:T(8,128)S(1)}, s32[2048]{0:T(1024)S(1)}, /*index...) while((s32[]{:T(128)}, f32[1,2048]{1,0:T(1,128)S(1)}, ...), condition=%wide.region_6.7_spmd.clone, body=%wide.region_3.0_spmd.clone.sunk | while | flops 768108544 | bytes 27504848 | solution.py:102
  172.8 5.7 %fusion.48 = (f32[2048]{0:T(1024)S(1)}, f32[1024,2048]{1,0:T(8,128)}) fusion(s32[2048]{0:T(1024)S(1)} %get-tuple-element.292, s32[1024]{0:T(1024)S(1)} %dynamic_slice.32, bf16[1,88,2048]{2,1,0:T(8,128)(2,1)S(1)} %get-tuple-element.295, bf16[2,88,16384]{2,1,0:T(8,128)(2,1)} %get-tuple-element.294, s32[]{:T(128)S(6)} %select_n.132), kind=kOutput, calls=%fused_computation.5.clone.1 | convolution fusion | flops 377485312 | bytes 8949764 | tf_op jit(solution)/shard_map/while/body/eval_jaxpr/hdq,hdk->hqk/dot_general | solution.py:70
  178.5 5.0 fusion.50
  183.5 5.5 %fusion.52 = f32[1,88,2048]{2,1,0:T(8,128)S(1)} fusion(f32[1024,2048]{1,0:T(8,128)} %get-tuple-element.259, f32[2048]{0:T(1024)S(1)} %bitcast.105, s32[2048]{0:T(1024)S(1)} %get-tuple-element.292, s32[1024]{0:T(1024)S(1)} %dynamic_slice.32, f32[1,88,2048]{2,1,0:T(8,128)S(1)} %get-tuple-element.278, f32[2048]{0:T(1024)S(1)} %bitcast.112, ...), kind=kOutput, calls=%fused_computation.12.clone.1 | convolution fusion | flops 380125184 | bytes 10039305 | tf_op jit(solution)/shard_map/while/body/eval_jaxpr/hqk,hdk->hdq/dot_general | solution.py:78
  189.1 5.5 %fusion.48 = (f32[2048]{0:T(1024)S(1)}, f32[1024,2048]{1,0:T(8,128)}) fusion(s32[2048]{0:T(1024)S(1)} %get-tuple-element.292, s32[1024]{0:T(1024)S(1)} %dynamic_slice.32, bf16[1,88,2048]{2,1,0:T(8,128)(2,1)S(1)} %get-tuple-element.295, bf16[2,88,16384]{2,1,0:T(8,128)(2,1)} %get-tuple-element.294, s32[]{:T(128)S(6)} %select_n.132), kind=kOutput, calls=%fused_computation.5.clone.1 | convolution fusion | flops 377485312 | bytes 8949764 | tf_op jit(solution)/shard_map/while/body/eval_jaxpr/hdq,hdk->hqk/dot_general | solution.py:70
  194.6 4.6 fusion.50
  199.3 5.4 %fusion.52 = f32[1,88,2048]{2,1,0:T(8,128)S(1)} fusion(f32[1024,2048]{1,0:T(8,128)} %get-tuple-element.259, f32[2048]{0:T(1024)S(1)} %bitcast.105, s32[2048]{0:T(1024)S(1)} %get-tuple-element.292, s32[1024]{0:T(1024)S(1)} %dynamic_slice.32, f32[1,88,2048]{2,1,0:T(8,128)S(1)} %get-tuple-element.278, f32[2048]{0:T(1024)S(1)} %bitcast.112, ...), kind=kOutput, calls=%fused_computation.12.clone.1 | convolution fusion | flops 380125184 | bytes 10039305 | tf_op jit(solution)/shard_map/while/body/eval_jaxpr/hqk,hdk->hdq/dot_general | solution.py:78
  204.7 6.2 %fusion.48 = (f32[2048]{0:T(1024)S(1)}, f32[1024,2048]{1,0:T(8,128)}) fusion(s32[2048]{0:T(1024)S(1)} %get-tuple-element.292, s32[1024]{0:T(1024)S(1)} %dynamic_slice.32, bf16[1,88,2048]{2,1,0:T(8,128)(2,1)S(1)} %get-tuple-element.295, bf16[2,88,16384]{2,1,0:T(8,128)(2,1)} %get-tuple-element.294, s32[]{:T(128)S(6)} %select_n.132), kind=kOutput, calls=%fused_computation.5.clone.1 | convolution fusion | flops 377485312 | bytes 8949764 | tf_op jit(solution)/shard_map/while/body/eval_jaxpr/hdq,hdk->hqk/dot_general | solution.py:70
  210.9 4.6 fusion.50
  215.6 5.6 %fusion.52 = f32[1,88,2048]{2,1,0:T(8,128)S(1)} fusion(f32[1024,2048]{1,0:T(8,128)} %get-tuple-element.259, f32[2048]{0:T(1024)S(1)} %bitcast.105, s32[2048]{0:T(1024)S(1)} %get-tuple-element.292, s32[1024]{0:T(1024)S(1)} %dynamic_slice.32, f32[1,88,2048]{2,1,0:T(8,128)S(1)} %get-tuple-element.278, f32[2048]{0:T(1024)S(1)} %bitcast.112, ...), kind=kOutput, calls=%fused_computation.12.clone.1 | convolution fusion | flops 380125184 | bytes 10039305 | tf_op jit(solution)/shard_map/while/body/eval_jaxpr/hqk,hdk->hdq/dot_general | solution.py:78
  221.2 5.5 %fusion.48 = (f32[2048]{0:T(1024)S(1)}, f32[1024,2048]{1,0:T(8,128)}) fusion(s32[2048]{0:T(1024)S(1)} %get-tuple-element.292, s32[1024]{0:T(1024)S(1)} %dynamic_slice.32, bf16[1,88,2048]{2,1,0:T(8,128)(2,1)S(1)} %get-tuple-element.295, bf16[2,88,16384]{2,1,0:T(8,128)(2,1)} %get-tuple-element.294, s32[]{:T(128)S(6)} %select_n.132), kind=kOutput, calls=%fused_computation.5.clone.1 | convolution fusion | flops 377485312 | bytes 8949764 | tf_op jit(solution)/shard_map/while/body/eval_jaxpr/hdq,hdk->hqk/dot_general | solution.py:70
  226.8 4.9 fusion.50
  231.7 5.7 %fusion.52 = f32[1,88,2048]{2,1,0:T(8,128)S(1)} fusion(f32[1024,2048]{1,0:T(8,128)} %get-tuple-element.259, f32[2048]{0:T(1024)S(1)} %bitcast.105, s32[2048]{0:T(1024)S(1)} %get-tuple-element.292, s32[1024]{0:T(1024)S(1)} %dynamic_slice.32, f32[1,88,2048]{2,1,0:T(8,128)S(1)} %get-tuple-element.278, f32[2048]{0:T(1024)S(1)} %bitcast.112, ...), kind=kOutput, calls=%fused_computation.12.clone.1 | convolution fusion | flops 380125184 | bytes 10039305 | tf_op jit(solution)/shard_map/while/body/eval_jaxpr/hqk,hdk->hdq/dot_general | solution.py:78
  237.4 5.5 %fusion.48 = (f32[2048]{0:T(1024)S(1)}, f32[1024,2048]{1,0:T(8,128)}) fusion(s32[2048]{0:T(1024)S(1)} %get-tuple-element.292, s32[1024]{0:T(1024)S(1)} %dynamic_slice.32, bf16[1,88,2048]{2,1,0:T(8,128)(2,1)S(1)} %get-tuple-element.295, bf16[2,88,16384]{2,1,0:T(8,128)(2,1)} %get-tuple-element.294, s32[]{:T(128)S(6)} %select_n.132), kind=kOutput, calls=%fused_computation.5.clone.1 | convolution fusion | flops 377485312 | bytes 8949764 | tf_op jit(solution)/shard_map/while/body/eval_jaxpr/hdq,hdk->hqk/dot_general | solution.py:70
  242.9 4.9 fusion.50
  247.9 5.7 %fusion.52 = f32[1,88,2048]{2,1,0:T(8,128)S(1)} fusion(f32[1024,2048]{1,0:T(8,128)} %get-tuple-element.259, f32[2048]{0:T(1024)S(1)} %bitcast.105, s32[2048]{0:T(1024)S(1)} %get-tuple-element.292, s32[1024]{0:T(1024)S(1)} %dynamic_slice.32, f32[1,88,2048]{2,1,0:T(8,128)S(1)} %get-tuple-element.278, f32[2048]{0:T(1024)S(1)} %bitcast.112, ...), kind=kOutput, calls=%fused_computation.12.clone.1 | convolution fusion | flops 380125184 | bytes 10039305 | tf_op jit(solution)/shard_map/while/body/eval_jaxpr/hqk,hdk->hdq/dot_general | solution.py:78
  253.6 5.5 %fusion.48 = (f32[2048]{0:T(1024)S(1)}, f32[1024,2048]{1,0:T(8,128)}) fusion(s32[2048]{0:T(1024)S(1)} %get-tuple-element.292, s32[1024]{0:T(1024)S(1)} %dynamic_slice.32, bf16[1,88,2048]{2,1,0:T(8,128)(2,1)S(1)} %get-tuple-element.295, bf16[2,88,16384]{2,1,0:T(8,128)(2,1)} %get-tuple-element.294, s32[]{:T(128)S(6)} %select_n.132), kind=kOutput, calls=%fused_computation.5.clone.1 | convolution fusion | flops 377485312 | bytes 8949764 | tf_op jit(solution)/shard_map/while/body/eval_jaxpr/hdq,hdk->hqk/dot_general | solution.py:70
  259.2 4.6 fusion.50
  263.8 5.4 %fusion.52 = f32[1,88,2048]{2,1,0:T(8,128)S(1)} fusion(f32[1024,2048]{1,0:T(8,128)} %get-tuple-element.259, f32[2048]{0:T(1024)S(1)} %bitcast.105, s32[2048]{0:T(1024)S(1)} %get-tuple-element.292, s32[1024]{0:T(1024)S(1)} %dynamic_slice.32, f32[1,88,2048]{2,1,0:T(8,128)S(1)} %get-tuple-element.278, f32[2048]{0:T(1024)S(1)} %bitcast.112, ...), kind=kOutput, calls=%fused_computation.12.clone.1 | convolution fusion | flops 380125184 | bytes 10039305 | tf_op jit(solution)/shard_map/while/body/eval_jaxpr/hqk,hdk->hdq/dot_general | solution.py:78
  269.2 5.5 %fusion.48 = (f32[2048]{0:T(1024)S(1)}, f32[1024,2048]{1,0:T(8,128)}) fusion(s32[2048]{0:T(1024)S(1)} %get-tuple-element.292, s32[1024]{0:T(1024)S(1)} %dynamic_slice.32, bf16[1,88,2048]{2,1,0:T(8,128)(2,1)S(1)} %get-tuple-element.295, bf16[2,88,16384]{2,1,0:T(8,128)(2,1)} %get-tuple-element.294, s32[]{:T(128)S(6)} %select_n.132), kind=kOutput, calls=%fused_computation.5.clone.1 | convolution fusion | flops 377485312 | bytes 8949764 | tf_op jit(solution)/shard_map/while/body/eval_jaxpr/hdq,hdk->hqk/dot_general | solution.py:70
  274.8 4.6 fusion.50
  279.4 5.4 %fusion.52 = f32[1,88,2048]{2,1,0:T(8,128)S(1)} fusion(f32[1024,2048]{1,0:T(8,128)} %get-tuple-element.259, f32[2048]{0:T(1024)S(1)} %bitcast.105, s32[2048]{0:T(1024)S(1)} %get-tuple-element.292, s32[1024]{0:T(1024)S(1)} %dynamic_slice.32, f32[1,88,2048]{2,1,0:T(8,128)S(1)} %get-tuple-element.278, f32[2048]{0:T(1024)S(1)} %bitcast.112, ...), kind=kOutput, calls=%fused_computation.12.clone.1 | convolution fusion | flops 380125184 | bytes 10039305 | tf_op jit(solution)/shard_map/while/body/eval_jaxpr/hqk,hdk->hdq/dot_general | solution.py:78
  284.9 5.5 %fusion.48 = (f32[2048]{0:T(1024)S(1)}, f32[1024,2048]{1,0:T(8,128)}) fusion(s32[2048]{0:T(1024)S(1)} %get-tuple-element.292, s32[1024]{0:T(1024)S(1)} %dynamic_slice.32, bf16[1,88,2048]{2,1,0:T(8,128)(2,1)S(1)} %get-tuple-element.295, bf16[2,88,16384]{2,1,0:T(8,128)(2,1)} %get-tuple-element.294, s32[]{:T(128)S(6)} %select_n.132), kind=kOutput, calls=%fused_computation.5.clone.1 | convolution fusion | flops 377485312 | bytes 8949764 | tf_op jit(solution)/shard_map/while/body/eval_jaxpr/hdq,hdk->hqk/dot_general | solution.py:70
  290.4 4.6 fusion.50
  295.0 5.4 %fusion.52 = f32[1,88,2048]{2,1,0:T(8,128)S(1)} fusion(f32[1024,2048]{1,0:T(8,128)} %get-tuple-element.259, f32[2048]{0:T(1024)S(1)} %bitcast.105, s32[2048]{0:T(1024)S(1)} %get-tuple-element.292, s32[1024]{0:T(1024)S(1)} %dynamic_slice.32, f32[1,88,2048]{2,1,0:T(8,128)S(1)} %get-tuple-element.278, f32[2048]{0:T(1024)S(1)} %bitcast.112, ...), kind=kOutput, calls=%fused_computation.12.clone.1 | convolution fusion | flops 380125184 | bytes 10039305 | tf_op jit(solution)/shard_map/while/body/eval_jaxpr/hqk,hdk->hdq/dot_general | solution.py:78
  300.5 5.5 %fusion.48 = (f32[2048]{0:T(1024)S(1)}, f32[1024,2048]{1,0:T(8,128)}) fusion(s32[2048]{0:T(1024)S(1)} %get-tuple-element.292, s32[1024]{0:T(1024)S(1)} %dynamic_slice.32, bf16[1,88,2048]{2,1,0:T(8,128)(2,1)S(1)} %get-tuple-element.295, bf16[2,88,16384]{2,1,0:T(8,128)(2,1)} %get-tuple-element.294, s32[]{:T(128)S(6)} %select_n.132), kind=kOutput, calls=%fused_computation.5.clone.1 | convolution fusion | flops 377485312 | bytes 8949764 | tf_op jit(solution)/shard_map/while/body/eval_jaxpr/hdq,hdk->hqk/dot_general | solution.py:70
  306.0 4.6 fusion.50
  310.6 5.4 %fusion.52 = f32[1,88,2048]{2,1,0:T(8,128)S(1)} fusion(f32[1024,2048]{1,0:T(8,128)} %get-tuple-element.259, f32[2048]{0:T(1024)S(1)} %bitcast.105, s32[2048]{0:T(1024)S(1)} %get-tuple-element.292, s32[1024]{0:T(1024)S(1)} %dynamic_slice.32, f32[1,88,2048]{2,1,0:T(8,128)S(1)} %get-tuple-element.278, f32[2048]{0:T(1024)S(1)} %bitcast.112, ...), kind=kOutput, calls=%fused_computation.12.clone.1 | convolution fusion | flops 380125184 | bytes 10039305 | tf_op jit(solution)/shard_map/while/body/eval_jaxpr/hqk,hdk->hdq/dot_general | solution.py:78
  316.1 5.5 %fusion.48 = (f32[2048]{0:T(1024)S(1)}, f32[1024,2048]{1,0:T(8,128)}) fusion(s32[2048]{0:T(1024)S(1)} %get-tuple-element.292, s32[1024]{0:T(1024)S(1)} %dynamic_slice.32, bf16[1,88,2048]{2,1,0:T(8,128)(2,1)S(1)} %get-tuple-element.295, bf16[2,88,16384]{2,1,0:T(8,128)(2,1)} %get-tuple-element.294, s32[]{:T(128)S(6)} %select_n.132), kind=kOutput, calls=%fused_computation.5.clone.1 | convolution fusion | flops 377485312 | bytes 8949764 | tf_op jit(solution)/shard_map/while/body/eval_jaxpr/hdq,hdk->hqk/dot_general | solution.py:70
  321.6 4.6 fusion.50
  326.2 5.4 %fusion.52 = f32[1,88,2048]{2,1,0:T(8,128)S(1)} fusion(f32[1024,2048]{1,0:T(8,128)} %get-tuple-element.259, f32[2048]{0:T(1024)S(1)} %bitcast.105, s32[2048]{0:T(1024)S(1)} %get-tuple-element.292, s32[1024]{0:T(1024)S(1)} %dynamic_slice.32, f32[1,88,2048]{2,1,0:T(8,128)S(1)} %get-tuple-element.278, f32[2048]{0:T(1024)S(1)} %bitcast.112, ...), kind=kOutput, calls=%fused_computation.12.clone.1 | convolution fusion | flops 380125184 | bytes 10039305 | tf_op jit(solution)/shard_map/while/body/eval_jaxpr/hqk,hdk->hdq/dot_general | solution.py:78
  331.7 5.5 %fusion.48 = (f32[2048]{0:T(1024)S(1)}, f32[1024,2048]{1,0:T(8,128)}) fusion(s32[2048]{0:T(1024)S(1)} %get-tuple-element.292, s32[1024]{0:T(1024)S(1)} %dynamic_slice.32, bf16[1,88,2048]{2,1,0:T(8,128)(2,1)S(1)} %get-tuple-element.295, bf16[2,88,16384]{2,1,0:T(8,128)(2,1)} %get-tuple-element.294, s32[]{:T(128)S(6)} %select_n.132), kind=kOutput, calls=%fused_computation.5.clone.1 | convolution fusion | flops 377485312 | bytes 8949764 | tf_op jit(solution)/shard_map/while/body/eval_jaxpr/hdq,hdk->hqk/dot_general | solution.py:70
  337.2 4.6 fusion.50
  341.9 5.4 %fusion.52 = f32[1,88,2048]{2,1,0:T(8,128)S(1)} fusion(f32[1024,2048]{1,0:T(8,128)} %get-tuple-element.259, f32[2048]{0:T(1024)S(1)} %bitcast.105, s32[2048]{0:T(1024)S(1)} %get-tuple-element.292, s32[1024]{0:T(1024)S(1)} %dynamic_slice.32, f32[1,88,2048]{2,1,0:T(8,128)S(1)} %get-tuple-element.278, f32[2048]{0:T(1024)S(1)} %bitcast.112, ...), kind=kOutput, calls=%fused_computation.12.clone.1 | convolution fusion | flops 380125184 | bytes 10039305 | tf_op jit(solution)/shard_map/while/body/eval_jaxpr/hqk,hdk->hdq/dot_general | solution.py:78
  347.3 5.5 %fusion.48 = (f32[2048]{0:T(1024)S(1)}, f32[1024,2048]{1,0:T(8,128)}) fusion(s32[2048]{0:T(1024)S(1)} %get-tuple-element.292, s32[1024]{0:T(1024)S(1)} %dynamic_slice.32, bf16[1,88,2048]{2,1,0:T(8,128)(2,1)S(1)} %get-tuple-element.295, bf16[2,88,16384]{2,1,0:T(8,128)(2,1)} %get-tuple-element.294, s32[]{:T(128)S(6)} %select_n.132), kind=kOutput, calls=%fused_computation.5.clone.1 | convolution fusion | flops 377485312 | bytes 8949764 | tf_op jit(solution)/shard_map/while/body/eval_jaxpr/hdq,hdk->hqk/dot_general | solution.py:70
  352.8 4.6 fusion.50
  357.5 5.4 %fusion.52 = f32[1,88,2048]{2,1,0:T(8,128)S(1)} fusion(f32[1024,2048]{1,0:T(8,128)} %get-tuple-element.259, f32[2048]{0:T(1024)S(1)} %bitcast.105, s32[2048]{0:T(1024)S(1)} %get-tuple-element.292, s32[1024]{0:T(1024)S(1)} %dynamic_slice.32, f32[1,88,2048]{2,1,0:T(8,128)S(1)} %get-tuple-element.278, f32[2048]{0:T(1024)S(1)} %bitcast.112, ...), kind=kOutput, calls=%fused_computation.12.clone.1 | convolution fusion | flops 380125184 | bytes 10039305 | tf_op jit(solution)/shard_map/while/body/eval_jaxpr/hqk,hdk->hdq/dot_general | solution.py:78
  362.9 5.5 %fusion.48 = (f32[2048]{0:T(1024)S(1)}, f32[1024,2048]{1,0:T(8,128)}) fusion(s32[2048]{0:T(1024)S(1)} %get-tuple-element.292, s32[1024]{0:T(1024)S(1)} %dynamic_slice.32, bf16[1,88,2048]{2,1,0:T(8,128)(2,1)S(1)} %get-tuple-element.295, bf16[2,88,16384]{2,1,0:T(8,128)(2,1)} %get-tuple-element.294, s32[]{:T(128)S(6)} %select_n.132), kind=kOutput, calls=%fused_computation.5.clone.1 | convolution fusion | flops 377485312 | bytes 8949764 | tf_op jit(solution)/shard_map/while/body/eval_jaxpr/hdq,hdk->hqk/dot_general | solution.py:70
  368.5 4.6 fusion.50
  373.1 5.4 %fusion.52 = f32[1,88,2048]{2,1,0:T(8,128)S(1)} fusion(f32[1024,2048]{1,0:T(8,128)} %get-tuple-element.259, f32[2048]{0:T(1024)S(1)} %bitcast.105, s32[2048]{0:T(1024)S(1)} %get-tuple-element.292, s32[1024]{0:T(1024)S(1)} %dynamic_slice.32, f32[1,88,2048]{2,1,0:T(8,128)S(1)} %get-tuple-element.278, f32[2048]{0:T(1024)S(1)} %bitcast.112, ...), kind=kOutput, calls=%fused_computation.12.clone.1 | convolution fusion | flops 380125184 | bytes 10039305 | tf_op jit(solution)/shard_map/while/body/eval_jaxpr/hqk,hdk->hdq/dot_general | solution.py:78
  378.5 5.5 %fusion.48 = (f32[2048]{0:T(1024)S(1)}, f32[1024,2048]{1,0:T(8,128)}) fusion(s32[2048]{0:T(1024)S(1)} %get-tuple-element.292, s32[1024]{0:T(1024)S(1)} %dynamic_slice.32, bf16[1,88,2048]{2,1,0:T(8,128)(2,1)S(1)} %get-tuple-element.295, bf16[2,88,16384]{2,1,0:T(8,128)(2,1)} %get-tuple-element.294, s32[]{:T(128)S(6)} %select_n.132), kind=kOutput, calls=%fused_computation.5.clone.1 | convolution fusion | flops 377485312 | bytes 8949764 | tf_op jit(solution)/shard_map/while/body/eval_jaxpr/hdq,hdk->hqk/dot_general | solution.py:70
  384.1 4.6 fusion.50
  388.7 5.4 %fusion.52 = f32[1,88,2048]{2,1,0:T(8,128)S(1)} fusion(f32[1024,2048]{1,0:T(8,128)} %get-tuple-element.259, f32[2048]{0:T(1024)S(1)} %bitcast.105, s32[2048]{0:T(1024)S(1)} %get-tuple-element.292, s32[1024]{0:T(1024)S(1)} %dynamic_slice.32, f32[1,88,2048]{2,1,0:T(8,128)S(1)} %get-tuple-element.278, f32[2048]{0:T(1024)S(1)} %bitcast.112, ...), kind=kOutput, calls=%fused_computation.12.clone.1 | convolution fusion | flops 380125184 | bytes 10039305 | tf_op jit(solution)/shard_map/while/body/eval_jaxpr/hqk,hdk->hdq/dot_general | solution.py:78
  394.1 5.5 %fusion.48 = (f32[2048]{0:T(1024)S(1)}, f32[1024,2048]{1,0:T(8,128)}) fusion(s32[2048]{0:T(1024)S(1)} %get-tuple-element.292, s32[1024]{0:T(1024)S(1)} %dynamic_slice.32, bf16[1,88,2048]{2,1,0:T(8,128)(2,1)S(1)} %get-tuple-element.295, bf16[2,88,16384]{2,1,0:T(8,128)(2,1)} %get-tuple-element.294, s32[]{:T(128)S(6)} %select_n.132), kind=kOutput, calls=%fused_computation.5.clone.1 | convolution fusion | flops 377485312 | bytes 8949764 | tf_op jit(solution)/shard_map/while/body/eval_jaxpr/hdq,hdk->hqk/dot_general | solution.py:70
  399.7 4.6 fusion.50
  404.3 5.4 %fusion.52 = f32[1,88,2048]{2,1,0:T(8,128)S(1)} fusion(f32[1024,2048]{1,0:T(8,128)} %get-tuple-element.259, f32[2048]{0:T(1024)S(1)} %bitcast.105, s32[2048]{0:T(1024)S(1)} %get-tuple-element.292, s32[1024]{0:T(1024)S(1)} %dynamic_slice.32, f32[1,88,2048]{2,1,0:T(8,128)S(1)} %get-tuple-element.278, f32[2048]{0:T(1024)S(1)} %bitcast.112, ...), kind=kOutput, calls=%fused_computation.12.clone.1 | convolution fusion | flops 380125184 | bytes 10039305 | tf_op jit(solution)/shard_map/while/body/eval_jaxpr/hqk,hdk->hdq/dot_general | solution.py:78
  409.8 5.5 %fusion.48 = (f32[2048]{0:T(1024)S(1)}, f32[1024,2048]{1,0:T(8,128)}) fusion(s32[2048]{0:T(1024)S(1)} %get-tuple-element.292, s32[1024]{0:T(1024)S(1)} %dynamic_slice.32, bf16[1,88,2048]{2,1,0:T(8,128)(2,1)S(1)} %get-tuple-element.295, bf16[2,88,16384]{2,1,0:T(8,128)(2,1)} %get-tuple-element.294, s32[]{:T(128)S(6)} %select_n.132), kind=kOutput, calls=%fused_computation.5.clone.1 | convolution fusion | flops 377485312 | bytes 8949764 | tf_op jit(solution)/shard_map/while/body/eval_jaxpr/hdq,hdk->hqk/dot_general | solution.py:70
  415.3 4.6 fusion.50
  419.9 5.4 %fusion.52 = f32[1,88,2048]{2,1,0:T(8,128)S(1)} fusion(f32[1024,2048]{1,0:T(8,128)} %get-tuple-element.259, f32[2048]{0:T(1024)S(1)} %bitcast.105, s32[2048]{0:T(1024)S(1)} %get-tuple-element.292, s32[1024]{0:T(1024)S(1)} %dynamic_slice.32, f32[1,88,2048]{2,1,0:T(8,128)S(1)} %get-tuple-element.278, f32[2048]{0:T(1024)S(1)} %bitcast.112, ...), kind=kOutput, calls=%fused_computation.12.clone.1 | convolution fusion | flops 380125184 | bytes 10039305 | tf_op jit(solution)/shard_map/while/body/eval_jaxpr/hqk,hdk->hdq/dot_general | solution.py:78
  426.3 6.4 %all-to-all-start = ((bf16[88,16,128]{2,0,1:T(8,128)(2,1)}), bf16[88,16,128]{2,0,1:T(8,128)(2,1)S(1)}, u32[]{:S(2)}, u32[]{:S(2)}) async-start(bf16[88,16,128]{2,0,1:T(8,128)(2,1)} %copy.35), calls=%async_computation | async-start | bytes 720896 | tf_op jit(solution)/shard_map/all_to_all | solution.py:107
  432.8 7.6 %convert_element_type.50 = f32[1408,2048]{0,1:T(8,128)} convert(bf16[1408,2048]{0,1:T(8,128)(2,1)} %copy.37) | non-fusion elementwise | flops 2883584 | bytes 17301504 | tf_op jit(solution)/shard_map/convert_element_type | solution.py:38
  442.6 3.2 fusion.35
  446.1 8.8 %fusion.27 = bf16[32,1408]{1,0:T(8,128)(2,1)} fusion(bf16[4,1408,1408]{2,1,0:T(8,128)(2,1)} %all-gather.9.cloned.1.call-done, bf16[1408,32,4]{0,2,1:T(4,128)(2,1)S(1)} %reshape.212), kind=kOutput, calls=%fused_computation.37 | convolution fusion | flops 507555840 | bytes 16310272 | tf_op jit(solution)/shard_map/fgi,ifd->gd/dot_general | solution.py:123
  456.4 41.4 %all-gather.11.cloned.1.call-done = bf16[512,1408]{1,0:T(8,128)(2,1)} async-done(((bf16[32,1408]{1,0:T(8,128)(2,1)}), bf16[512,1408]{1,0:T(8,128)(2,1)}) %all-gather.11.cloned.1.call-update) | async-done | bytes 1441808 | tf_op jit(solution)/shard_map/all_gather | solution.py:124
  (115 shorter events, 20.0 us)
Async XLA Ops:
  6.5 110.4 %copy-start = (bf16[2,88,1408]{2,1,0:T(8,128)(2,1)S(1)}, bf16[2,88,1408]{2,1,0:T(8,128)(2,1)}, u32[]{:S(2)}) copy-start(bf16[2,88,1408]{2,1,0:T(8,128)(2,1)} %param.16) | copy-start | bytes 1486852
  6.5 82.5 %all-gather.5.cloned.1.call-start = ((), (), s32[]{:S(2)}) async-start(), calls=%async_computation.1 | async-start | bytes 10340352 | tf_op jit(solution)/shard_map/all_gather | solution.py:34
  8.6 157.4 %all-gather.7.cloned.1.call-start = ((), (), s32[]{:S(2)}) async-start(), calls=%async_computation.2 | async-start | bytes 6782976 | tf_op jit(solution)/shard_map/all_gather | solution.py:61
  103.5 4.5 copy-start.2
  111.9 14.4 %copy-start.4 = (bf16[88,1408]{1,0:T(8,128)(2,1)S(1)}, bf16[88,1408]{1,0:T(8,128)(2,1)}, u32[]{:S(2)}) copy-start(bf16[88,1408]{1,0:T(8,128)(2,1)} %param.15) | copy-start | bytes 743428
  126.1 320.0 %all-gather.9.cloned.1.call-start = ((), (), s32[]{:S(2)}) async-start(), calls=%async_computation.3 | async-start | bytes 16850944 | tf_op jit(solution)/shard_map/all_gather | solution.py:121
  126.4 46.4 %copy-start.3 = (s32[2048]{0:T(1024)S(1)}, s32[2048]{0:T(1024)}, u32[]{:S(2)}) copy-start(s32[2048]{0:T(1024)} %param.19) | copy-start | bytes 24580
  172.7 260.0 %copy-start.5 = (bf16[1408]{0:T(1024)(128)(2,1)S(1)}, bf16[1408]{0:T(1024)(128)(2,1)}, u32[]{:S(2)}) copy-start(bf16[1408]{0:T(1024)(128)(2,1)} %param.21) | copy-start | bytes 8452
  426.3 16.2 %all-to-all-start = ((bf16[88,16,128]{2,0,1:T(8,128)(2,1)}), bf16[88,16,128]{2,0,1:T(8,128)(2,1)S(1)}, u32[]{:S(2)}, u32[]{:S(2)}) async-start(bf16[88,16,128]{2,0,1:T(8,128)(2,1)} %copy.35), calls=%async_computation | async-start | bytes 720896 | tf_op jit(solution)/shard_map/all_to_all | solution.py:107
  432.7 65.0 %all-gather.11.cloned.1.call-start = ((), (), s32[]{:S(2)}) async-start(), calls=%async_computation.4 | async-start | bytes 1531904 | tf_op jit(solution)/shard_map/all_gather | solution.py:124
  446.0 55.1 %copy-start.1 = (bf16[2,88,1408]{2,1,0:T(8,128)(2,1)S(1)}, bf16[2,88,1408]{2,1,0:T(8,128)(2,1)}, u32[]{:S(2)}) copy-start(bf16[2,88,1408]{2,1,0:T(8,128)(2,1)} %param.16) | copy-start | bytes 1486852
Sparse Core Ops, SparseCore 0:
  9.5 79.4 all-gather.4
  126.2 39.7 all-gather.6
  168.2 106.3 all-gather.8
  455.1 42.6 all-gather.10
